TPU v7x, 512 devices: a whole 4x4x16 slice. The times are simulated.
512 devices in a mesh: cols: 128 (over x, z, core), edge: 4 (over y).
Axes of the slice: x: 4, y: 4, z: 16, core: 2. Of those that a mesh axis runs over, the one named last changes fastest.
Arguments:
- state: float32 [4, 16384, 512], P('edge', 'cols'), may hold values from -6 to 6
- owners: int32 [4, 16384, 1], P('edge', 'cols'), may hold values from 0 to 127; in each aligned block of 128 rows (0 to 127, 128 to 255, ..., all dimensions but the last counted through in order) at most 2 rows name the same one
- orient: int32 [4, 128, 2], P('edge', 'cols'), may hold values from 0 to 1
- crm_state: bfloat16 [4, 128, 58, 16384], P('edge', 'cols'), may hold values from -6 to 6
- active_levels: int32 [4, 128, 256], P('edge', 'cols'), may hold values from 14 to 58
- vertical_map: float32 [58, 64], replicated, may hold values from -0.75 to 0.75
- diffusion: float32 [57], replicated, may hold values from 0.1 to 4
Outputs:
- new_state: float32 [4, 16384, 512], P('edge', 'cols')
- crm_out: bfloat16 [4, 128, 58, 16384], P('edge', 'cols')
Inputs may be any that keep to these rules, and one draw needn't show every extreme that they name: `owners`: within the columns of one tile no group is named more than 2 times.
All inputs are finite; a program needn't handle non-finite values.
Results may differ from a plain program's by a relative error of at most 0.001.
Values sent between devices are 32-bit elements; how exact they have to be, the bound alone decides.
A program may use at most 64 MiB of HBM per device.

v0:
```python
import jax
import jax.numpy as jnp
from jax import lax
from jax.sharding import PartitionSpec as P

L = 64
CX = 64
CZ = 58
TW = 8
SUBSTEPS = 2


kappa_edge = 0.25
max_courant = 0.9
relax_rate = 0.5


def from_behind(value, axis, steps):
    count = lax.axis_size(axis)
    pairs = [(source, (source + steps) % count) for source in range(count)]
    return lax.ppermute(value, axis, pairs)


def factorize(lower, diagonal, upper):
    depth = diagonal.shape[0]
    prev_c = jnp.zeros(diagonal.shape[1:], jnp.float32)
    factors = []
    denoms = []
    for level in range(depth):
        denom = diagonal[level] + lower[level] * prev_c
        prev_c = -upper[level] / denom
        factors.append(prev_c)
        denoms.append(denom)
    return (factors, denoms)


def tridiag(lower, factors, denoms, values):
    depth = values.shape[0]
    prev_d = jnp.zeros(values.shape[1:], jnp.float32)
    offsets = []
    for level in range(depth):
        prev_d = (values[level] + lower[level][None, :] * prev_d) / denoms[level][None, :]
        offsets.append(prev_d)
    after = jnp.zeros(values.shape[1:], jnp.float32)
    solved = [None] * depth
    for level in range(depth - 1, -1, -1):
        after = offsets[level] - factors[level][None, :] * after
        solved[level] = after
    return jnp.stack(solved, axis=0)


def physics(columns, crm_slab, active_count, vertical_map, diffusion):
    slots = columns.shape[0]
    temper = columns[:, 0:L]
    moisture = columns[:, L : 2 * L]
    forcing = jnp.einsum(
        "zl,sl->zs",
        vertical_map,
        temper,
        precision=lax.Precision.HIGHEST,
        preferred_element_type=jnp.float32,
    )
    courant = max_courant * jax.nn.sigmoid(
        jnp.einsum(
            "zl,sl->zs",
            vertical_map,
            moisture,
            precision=lax.Precision.HIGHEST,
            preferred_element_type=jnp.float32,
        )
    )
    field = crm_slab.reshape(CZ, CX, slots).astype(jnp.float32)
    mean_before = jnp.mean(field, axis=1)
    spread_before = jnp.mean(field * field, axis=1) - mean_before * mean_before
    field = field + relax_rate * (forcing - mean_before)[:, None, :]
    heights = jnp.arange(CZ - 1, dtype=jnp.int32)
    coupled = (heights[:, None] + 1 < active_count[None, :]).astype(jnp.float32)
    interfaces = diffusion[:, None] * coupled
    zero_row = jnp.zeros((1, slots), jnp.float32)
    lower = jnp.concatenate([zero_row, interfaces], axis=0)
    upper = jnp.concatenate([interfaces, zero_row], axis=0)
    diagonal = 1.0 + lower + upper
    factors, denoms = factorize(lower, diagonal, upper)
    for substep in range(SUBSTEPS):
        field = field - courant[:, None, :] * (field - jnp.roll(field, 1, axis=1))
        field = tridiag(lower, factors, denoms, field)
    mean_after = jnp.mean(field, axis=1)
    spread_after = jnp.mean(field * field, axis=1) - mean_after * mean_after
    tend_mean = jnp.einsum(
        "zs,zl->sl",
        mean_after - mean_before,
        vertical_map,
        precision=lax.Precision.HIGHEST,
        preferred_element_type=jnp.float32,
    )
    tend_spread = jnp.einsum(
        "zs,zl->sl",
        spread_after - spread_before,
        vertical_map,
        precision=lax.Precision.HIGHEST,
        preferred_element_type=jnp.float32,
    )
    tend = jnp.concatenate([tend_mean, tend_spread], axis=1)
    return (tend, field.reshape(CZ, CX * slots).astype(jnp.bfloat16))


def shards(state, owners, orient, crm_state, active_levels, vertical_map, diffusion):
    n_tiles = lax.axis_size("cols")
    per_tile = state.shape[1]
    width = state.shape[2]
    cap_slots = max(2, 2 * per_tile // n_tiles)
    rows_along = per_tile // TW
    tiles = state[0].reshape(rows_along, TW, width)
    upper_row = tiles[rows_along - 1]
    lower_row = tiles[0]
    ghost_low = from_behind(upper_row, "edge", 1)
    ghost_high = from_behind(lower_row, "edge", -1)
    flags = orient[0, 0]
    ghost_low = jnp.where(flags[0] == 1, ghost_low[::-1], ghost_low)
    ghost_high = jnp.where(flags[1] == 1, ghost_high[::-1], ghost_high)
    padded = jnp.concatenate([ghost_low[None], tiles, ghost_high[None]], axis=0)
    moved = tiles + kappa_edge * (padded[2:] + padded[:-2] - 2.0 * tiles)
    moved = moved.reshape(per_tile, width)
    group_of = owners[0, :, 0]
    same = group_of[:, None] == group_of[None, :]
    order = jnp.arange(per_tile, dtype=jnp.int32)
    earlier = order[None, :] < order[:, None]
    ranking = jnp.sum((same & earlier).astype(jnp.int32), axis=1)
    slot_index = group_of * cap_slots + ranking
    outgoing = (
        jnp.zeros((n_tiles * cap_slots, moved.shape[1]), jnp.float32).at[slot_index].set(moved)
    )
    received = lax.all_to_all(outgoing, "cols", split_axis=0, concat_axis=0, tiled=True)
    tend, crm_new = physics(received, crm_state[0, 0], active_levels[0, 0], vertical_map, diffusion)
    updated = received[:, 0 : 2 * L] + tend
    reply = jnp.concatenate([updated, received[:, 2 * L :]], axis=1)
    returned = lax.all_to_all(reply, "cols", split_axis=0, concat_axis=0, tiled=True)
    gathered = returned[slot_index]
    return (gathered[None], crm_new[None, None])


def solution(mesh):
    in_specs = (
        P("edge", "cols", None),
        P("edge", "cols", None),
        P("edge", "cols", None),
        P("edge", "cols", None, None),
        P("edge", "cols", None),
        P(),
        P(),
    )
    out_specs = (P("edge", "cols", None), P("edge", "cols", None, None))
    return jax.shard_map(shards, mesh=mesh, in_specs=in_specs, out_specs=out_specs, check_vma=False)
```

profile of v0, /device:TPU:7, one launch (start us, length us, event | category | flops | bytes accessed | tf_op | source)
XLA Modules:
  0.0 140.8 jit_solution(11141163712329348824)
XLA Ops:
  1.4 4.6 %collective-permute-start = (f32[8,512]{1,0:T(8,128)S(1)}, f32[8,512]{1,0:T(8,128)S(1)}, u32[]{:S(2)}, u32[]{:S(2)}) collective-permute-start(f32[8,512]{1,0:T(8,128)S(1)} %get-tuple-element.318), channel_id=1, source_target_pairs={{0,3},{1,0},{2,1},{3,2},{4,7},{5,4},{6,5},{7,6},{8,11},{9,8},{10,9... | collective-permute-start | bytes 49160 | tf_op jit(solution)/shard_map/ppermute | solution.py:21
  6.0 1.9 %collective-permute-start.1 = (f32[8,512]{1,0:T(8,128)S(1)}, f32[8,512]{1,0:T(8,128)S(1)}, u32[]{:S(2)}, u32[]{:S(2)}) collective-permute-start(f32[8,512]{1,0:T(8,128)S(1)} %get-tuple-element.319), channel_id=1, source_target_pairs={{0,1},{1,2},{2,3},{3,0},{4,5},{5,6},{6,7},{7,4},{8,9},{9,10},{10,1... | collective-permute-start | bytes 49160 | tf_op jit(solution)/shard_map/ppermute | solution.py:21
  10.4 1.3 fusion.330
  13.0 1.9 %convert_element_type.29 = f32[1,1,58,16384]{3,2,1,0:T(8,128)S(1)} convert(bf16[1,1,58,16384]{3,2,1,0:T(8,128)(2,1)} %param.10) | non-fusion elementwise | flops 950272 | bytes 5701632 | tf_op jit(solution)/shard_map/convert_element_type | solution.py:72
  14.9 3.2 %copy.16 = f32[8,8,64,256]{3,2,1,0:T(8,128)} copy(f32[8,8,64,256]{3,1,2,0:T(8,128)S(1)} %bitcast.1257) | data formatting | bytes 8388608
  18.3 1.2 scatter_custom_fusion
  19.5 1.1 all_to_all.16
  20.6 20.7 %all-to-all-start = ((f32[128,2,512]{2,1,0:T(2,128)}), f32[128,2,512]{2,1,0:T(2,128)S(1)}, u32[]{:S(2)}, u32[]{:S(2)}) async-start(f32[128,2,512]{2,1,0:T(2,128)} %all_to_all.16), calls=%async_computation | async-start | bytes 1048576 | tf_op jit(solution)/shard_map/all_to_all | solution.py:133
  42.5 3.2 %slice_reduce_fusion = (f32[58,256]{1,0:T(8,128)S(1)}, f32[58,256]{1,0:T(8,128)S(1)}) fusion(f32[64,64,256]{2,1,0:T(8,128)} %bitcast.1254), kind=kLoop, calls=%fused_computation.11 | loop fusion | flops 2821120 | bytes 3919872 | tf_op jit(solution)/shard_map/reduce_sum | solution.py:73
  45.7 26.3 %all-to-all-done = f32[128,2,512]{2,1,0:T(2,128)S(1)} async-done(((f32[128,2,512]{2,1,0:T(2,128)}), f32[128,2,512]{2,1,0:T(2,128)S(1)}, u32[]{:S(2)}, u32[]{:S(2)}) %all-to-all-start) | async-done | bytes 524320 | tf_op jit(solution)/shard_map/all_to_all | solution.py:133
  73.0 2.7 %slice_add_fusion = f32[58,64,256]{2,1,0:T(8,128)S(1)} fusion(f32[64,64,256]{2,1,0:T(8,128)} %bitcast.1255, f32[58,256]{1,0:T(8,128)S(1)} %fusion.10), kind=kLoop, calls=%fused_computation.10 | loop fusion | flops 950272 | bytes 7661568 | tf_op jit(solution)/shard_map/add | solution.py:75
  76.3 1.5 %fusion.1 = f32[58,64,256]{2,1,0:T(8,128)S(1)} fusion(f32[58,63,256]{2,1,0:T(8,128)S(1)} %bitcast.1259, f32[58,1,256]{2,1,0:T(1,128)S(1)} %slice.1164, f32[58,256]{1,0:T(8,128)S(1)} %fusion.8, f32[58,256]{1,0:T(8,128)S(1)} %fusion.10, f32[64,64,256]{2,1,0:T(8,128)S(1)} %bitcast.1256), kind=kLoop, calls=%fused_computation.4 | loop fusion | flops 4751360 | bytes 11522048 | tf_op jit(solution)/shard_map/sub | solution.py:85
  77.8 1.0 constant_dynamic-update-slice_fusion.57
  79.5 1.0 constant_dynamic-update-slice_fusion.14
  80.8 1.4 fusion.3
  93.5 1.4 %fusion.252 = (f32[58,256]{1,0:T(8,128)S(1)}, f32[58,256]{1,0:T(8,128)S(1)}) fusion(f32[58,64,256]{2,1,0:T(8,128)S(1)} %constant_dynamic-update-slice_fusion.58), kind=kLoop, calls=%fused_computation.776 | loop fusion | flops 2821120 | bytes 3919872 | tf_op jit(solution)/shard_map/reduce_sum | solution.py:87
  95.8 1.1 all_to_all.19
  96.9 9.5 %all-to-all-start.1 = ((f32[128,2,512]{2,1,0:T(2,128)}), f32[128,2,512]{2,1,0:T(2,128)S(1)}, u32[]{:S(2)}, u32[]{:S(2)}) async-start(f32[128,2,512]{2,1,0:T(2,128)} %all_to_all.19), calls=%async_computation.1 | async-start | bytes 1048576 | tf_op jit(solution)/shard_map/all_to_all | solution.py:137
  108.2 1.4 stack.362
  109.6 1.4 stack.363
  111.0 1.4 stack.364
  112.4 1.4 stack.365
  113.8 1.4 stack.366
  115.2 1.4 stack.367
  116.6 1.4 stack.368
  118.0 1.4 stack.369
  119.4 1.4 stack.370
  120.8 1.4 stack.371
  122.2 1.4 stack.372
  123.6 1.4 stack.373
  125.6 13.4 %stack.390 = bf16[1,1,58,16384]{3,2,1,0:T(8,128)(2,1)} concatenate(bf16[1,1,1,16384]{3,2,1,0:T(2,128)(2,1)S(1)} %stack.332, bf16[1,1,1,16384]{3,2,1,0:T(2,128)(2,1)S(1)} %stack.333, bf16[1,1,1,16384]{3,2,1,0:T(2,128)(2,1)S(1)} %stack.334, bf16[1,1,1,16384]{3,2,1,0:T(2,128)(2,1)S(1)} %stack.335, bf16[1,1,1,16384]{3,2,1,0:T(2,128)(2,1)S(1)} %stack.336, ...), dimensions={2} | concatenate | bytes 3801088 | tf_op jit(solution)/shard_map/stack | solution.py:49
  139.4 1.5 %gather_fusion = f32[128,512]{1,0:T(8,128)} fusion(f32[256,512]{1,0:T(8,128)S(1)} %all_to_all.21, s32[1024]{0:T(1024)S(1)} %pad_clamp_fusion), kind=kCustom, calls=%fused_computation | custom fusion | bytes 524800 | tf_op jit(solution)/shard_map/gather | solution.py:138
  (265 shorter events, 20.6 us)
Async XLA Ops:
  0.6 71.7 %copy-start = (f32[58,64]{1,0:T(8,128)S(1)}, f32[58,64]{1,0:T(8,128)}, u32[]{:S(2)}) copy-start(f32[58,64]{1,0:T(8,128)} %param.12) | copy-start | bytes 44548
  1.4 16.7 %collective-permute-start = (f32[8,512]{1,0:T(8,128)S(1)}, f32[8,512]{1,0:T(8,128)S(1)}, u32[]{:S(2)}, u32[]{:S(2)}) collective-permute-start(f32[8,512]{1,0:T(8,128)S(1)} %get-tuple-element.318), channel_id=1, source_target_pairs={{0,3},{1,0},{2,1},{3,2},{4,7},{5,4},{6,5},{7,6},{8,11},{9,8},{10,9... | collective-permute-start | bytes 49160 | tf_op jit(solution)/shard_map/ppermute | solution.py:21
  6.0 12.2 %collective-permute-start.1 = (f32[8,512]{1,0:T(8,128)S(1)}, f32[8,512]{1,0:T(8,128)S(1)}, u32[]{:S(2)}, u32[]{:S(2)}) collective-permute-start(f32[8,512]{1,0:T(8,128)S(1)} %get-tuple-element.319), channel_id=1, source_target_pairs={{0,1},{1,2},{2,3},{3,0},{4,5},{5,6},{6,7},{7,4},{8,9},{9,10},{10,1... | collective-permute-start | bytes 49160 | tf_op jit(solution)/shard_map/ppermute | solution.py:21
  14.9 3.5 %copy-start.3 = (f32[1,128,512]{2,1,0:T(8,128)S(1)}, f32[1,128,512]{2,1,0:T(8,128)}, u32[]{:S(2)}) copy-start(f32[1,128,512]{2,1,0:T(8,128)} %param.7) | copy-start | bytes 786436
  20.6 51.4 %all-to-all-start = ((f32[128,2,512]{2,1,0:T(2,128)}), f32[128,2,512]{2,1,0:T(2,128)S(1)}, u32[]{:S(2)}, u32[]{:S(2)}) async-start(f32[128,2,512]{2,1,0:T(2,128)} %all_to_all.16), calls=%async_computation | async-start | bytes 1048576 | tf_op jit(solution)/shard_map/all_to_all | solution.py:133
  72.4 11.0 %copy-start.2 = (f32[256,512]{1,0:T(8,128)}, f32[256,512]{1,0:T(8,128)S(1)}, u32[]{:S(2)}) copy-start(f32[256,512]{1,0:T(8,128)S(1)} %all_to_all.18) | copy-start | bytes 1572868
  73.0 3.3 %copy-start.1 = (f32[8,8,64,256]{3,2,1,0:T(8,128)S(1)}, f32[8,8,64,256]{3,2,1,0:T(8,128)}, u32[]{:S(2)}) copy-start(f32[8,8,64,256]{3,2,1,0:T(8,128)} %copy.16) | copy-start | bytes 12582916
  93.1 2.1 %slice-start = ((f32[256,512]{1,0:T(8,128)}), f32[256,128]{1,0:T(8,128)S(1)}, s32[]{:S(2)}) async-start(f32[256,512]{1,0:T(8,128)} %copy-done.2), calls=%async_computation.2 | async-start | bytes 262144 | tf_op jit(solution)/shard_map/slice | solution.py:135
  93.3 2.4 %slice-start.1 = ((f32[256,512]{1,0:T(8,128)}), f32[256,384]{1,0:T(8,128)S(1)}, s32[]{:S(2)}) async-start(f32[256,512]{1,0:T(8,128)} %copy-done.2), calls=%async_computation.3 | async-start | bytes 786432 | tf_op jit(solution)/shard_map/slice | solution.py:136
  96.9 42.1 %all-to-all-start.1 = ((f32[128,2,512]{2,1,0:T(2,128)}), f32[128,2,512]{2,1,0:T(2,128)S(1)}, u32[]{:S(2)}, u32[]{:S(2)}) async-start(f32[128,2,512]{2,1,0:T(2,128)} %all_to_all.19), calls=%async_computation.1 | async-start | bytes 1048576 | tf_op jit(solution)/shard_map/all_to_all | solution.py:137
where the time goes:
time: 143 us; the launch traced here: 141 us
  local copies, waits for them, and re-layouts  43.8 us (31%)
  starting transfers between devices  36.7 us (26%)
  other arithmetic  29.3 us (20%)
  waiting for transfers between devices  26.3 us (18%)
  between operations  3.69 us (3%)
    another operation x60, local copies, waits for them, and re-layouts, tridiag(): return jnp.stack(solved, axis=0)  32.4 us
    all_to_all x1, waiting for transfers between devices, shards(): lax.all_to_all(outgoing, 'cols', split_axis=0, concat_axis=0, tiled=True)  26.3 us
    all_to_all x1, starting transfers between devices, shards(): lax.all_to_all(outgoing, 'cols', split_axis=0, concat_axis=0, tiled=True)  20.7 us
    another operation x58, other arithmetic  10.2 us
    all_to_all x1, starting transfers between devices, shards(): lax.all_to_all(reply, 'cols', split_axis=0, concat_axis=0, tiled=True)  9.47 us
    ppermute x2, starting transfers between devices, from_behind(): return lax.ppermute(value, axis, pairs)  6.55 us
    unnamed x92, local copies, waits for them, and re-layouts  4.46 us
    reduce_sum x1, other arithmetic, physics(): mean_before = jnp.mean(field, axis=1)  3.24 us
  transfers between devices with their start and end apart: 4, of which 1 were waited for; matrix products, arithmetic and copies ran while one was open for 32% of the time, Pallas kernels for 0%

commit v1 on v0

v1 whole, which is shorter than its diff:
```python
import functools

import jax
import jax.numpy as jnp
from jax import lax
from jax.experimental import pallas as pl
from jax.experimental.pallas import tpu as pltpu
from jax.sharding import PartitionSpec as P

MESH = pl.DeviceIdType.MESH

L = 64
CX = 64
CZ = 58
TW = 8
CPD = 128
FL = 512
SLOTS = 256
HALF = 128
N = 128
NX, NZ, NC, NE = 4, 16, 2, 4
ZROWS = 64
HROWS = ZROWS * CX

kappa_edge = 0.25
max_courant = 0.9
relax_rate = 0.5

HIGHEST = lax.Precision.HIGHEST


def index_of(x, z, core):
    return (x * NZ + z) * NC + core


def around(value, count):
    return lax.rem(value + count, count)


def split(values):
    high = values.astype(jnp.bfloat16)
    low = (values - high.astype(jnp.float32)).astype(jnp.bfloat16)
    return jnp.concatenate([high, low], axis=1)


def kernel(
    state_hbm, owners_hbm, orient_hbm, crm_hbm, active_hbm, vmap_hbm, diff_hbm,
    new_hbm, out_hbm,
    tile, ghosts, owner, active, vmap, orient, diff, crm, field,
    rl, cl, el, ru, cu, eu, a1, b1, d1, a2, b2, mean, spread, part, partsq,
    weights, delta, moved, send, recv, reply, ret,
    ready, load_sem, crm_sem, halo_send, halo_recv, fwd_send, fwd_recv, rep_send, rep_recv, store_sem, crm_out_sem,
):
    me = lax.axis_index("cols")
    strip = lax.axis_index("edge")
    x = me // (NZ * NC)
    z = lax.rem(me // NC, NZ)
    core = lax.rem(me, NC)
    above = around(strip + 1, NE)
    below = around(strip - 1, NE)

    barrier = pltpu.get_barrier_semaphore()

    def greet(column, row):
        pl.semaphore_signal(barrier, inc=1, device_id=(column, row), device_id_type=MESH)

    def greet_ring(i, carry):
        greet(index_of(x, around(z + i, NZ), core), strip)
        return carry

    def plane_peer(i):
        i = i + core + NC * x
        return index_of(lax.rem(i // NC, NX), z, lax.rem(i, NC))

    def greet_plane(i, carry):
        greet(plane_peer(i), strip)
        return carry

    lax.fori_loop(1, NZ, greet_ring, 0)
    lax.fori_loop(1, NX * NC, greet_plane, 0)
    greet(me, above)
    greet(me, below)

    loads = [
        pltpu.make_async_copy(state_hbm.at[0], tile.at[pl.ds(TW, CPD)], load_sem.at[0]),
        pltpu.make_async_copy(owners_hbm, owner, load_sem.at[1]),
        pltpu.make_async_copy(active_hbm, active, load_sem.at[2]),
        pltpu.make_async_copy(vmap_hbm, vmap, load_sem.at[3]),
        pltpu.make_async_copy(orient_hbm, orient, load_sem.at[4]),
        pltpu.make_async_copy(diff_hbm, diff, load_sem.at[5]),
    ]
    for load in loads:
        load.start()
    pieces = 4
    width = CX * SLOTS // pieces
    crm_loads = [
        pltpu.make_async_copy(
            crm_hbm.at[0, 0, :, pl.ds(i * width, width)], crm.at[:, pl.ds(i * width, width)], crm_sem.at[i]
        )
        for i in range(pieces)
    ]
    for load in crm_loads:
        load.start()
    for load in loads:
        load.wait()

    count = active[...]

    def put(ref, level, values):
        for half in range(2):
            ref[pl.ds(half * ZROWS + level, 1), :] = values[:, half * HALF : (half + 1) * HALF]

    def factor(i, carry):
        lower_e, upper_e, k_before, k_after = carry
        level = i
        k_here = jnp.where(level + 1 < count, diff[0, jnp.minimum(level, CZ - 2)], 0.0)
        k_here = jnp.where(level < CZ - 1, k_here, 0.0)
        inv = 1.0 / (1.0 + k_before + k_here - k_before * lower_e)
        lower_e = k_here * inv
        put(rl, level, inv)
        put(cl, level, k_before * inv)
        put(el, level, lower_e)
        top = CZ - 1 - i
        k_under = jnp.where(top < count, diff[0, jnp.maximum(top - 1, 0)], 0.0)
        k_under = jnp.where(top > 0, k_under, 0.0)
        inv_u = 1.0 / (1.0 + k_after + k_under - k_after * upper_e)
        upper_e = k_under * inv_u
        put(ru, top, inv_u)
        put(cu, top, k_after * inv_u)
        put(eu, top, upper_e)
        return lower_e, upper_e, k_here, k_under

    zero_row = jnp.zeros((1, SLOTS), jnp.float32)
    lax.fori_loop(0, CZ, factor, (zero_row, zero_row, zero_row, zero_row))

    weights[...] = jnp.zeros((CPD, CPD), jnp.float32)
    weights[0:CZ, 0:L] = vmap[...]
    weights[L : L + CZ, L : 2 * L] = vmap[...]
    delta[...] = jnp.zeros((CPD, SLOTS), jnp.float32)

    sums = tuple(jnp.zeros((CZ, HALF), jnp.float32) for _ in range(4))

    def relayout(column, carry):
        carry = list(carry)
        spot = lax.rem(column, 8) * 8 + column // 8
        for half in range(2):
            start = pl.multiple_of(column * SLOTS + half * HALF, HALF)
            values = crm[:, pl.ds(start, HALF)].astype(jnp.float32)
            carry[half] = carry[half] + values
            carry[2 + half] = carry[2 + half] + values * values
            for block in range(ZROWS // 8):
                rows = min(8, CZ - 8 * block)
                field[pl.ds(half * HROWS + block * 8 * CX + spot, rows, stride=CX), :] = values[8 * block : 8 * block + rows]
        return tuple(carry)

    for i in range(pieces):
        crm_loads[i].wait()
        sums = lax.fori_loop(i * CX // pieces, (i + 1) * CX // pieces, relayout, sums)
    for half in range(2):
        levels = slice(half * ZROWS, half * ZROWS + CZ)
        average = sums[half] * (1.0 / CX)
        mean[levels, :] = average
        spread[levels, :] = sums[2 + half] * (1.0 / CX) - average * average

    group = owner[...]
    line = lax.broadcasted_iota(jnp.int32, (CPD, CPD), 0)
    along = lax.broadcasted_iota(jnp.int32, (CPD, CPD), 1)
    named = jnp.where(line == group, 1.0, 0.0)
    earlier = jnp.where(line < along, 1.0, 0.0)
    before = jnp.dot(named.astype(jnp.bfloat16), earlier.astype(jnp.bfloat16), preferred_element_type=jnp.float32)
    rank = jnp.sum(named * before, axis=0, keepdims=True)
    slot = group * 2 + rank.astype(jnp.int32)
    picks = jnp.where(lax.broadcasted_iota(jnp.int32, (SLOTS, CPD), 0) == slot, 1.0, 0.0).astype(jnp.bfloat16)

    pl.semaphore_wait(barrier, NZ - 1 + NX * NC - 1 + 2)

    def announce(i, carry):
        pl.semaphore_signal(ready, inc=1, device_id=(plane_peer(i), strip), device_id_type=MESH)
        return carry

    upward = pltpu.make_async_remote_copy(
        state_hbm.at[0, pl.ds(CPD - TW, TW)], ghosts.at[0], halo_send.at[0], halo_recv.at[0],
        device_id=(me, above), device_id_type=MESH,
    )
    downward = pltpu.make_async_remote_copy(
        state_hbm.at[0, pl.ds(0, TW)], ghosts.at[1], halo_send.at[1], halo_recv.at[1],
        device_id=(me, below), device_id_type=MESH,
    )
    upward.start()
    downward.start()
    lax.fori_loop(1, NX * NC, announce, 0)
    upward.wait()
    downward.wait()
    for side in range(2):
        flip = orient[0, side] == 1
        for w in range(TW):
            row = side * (TW + CPD) + w
            tile[row : row + 1, :] = jnp.where(flip, ghosts[side, TW - 1 - w : TW - w, :], ghosts[side, w : w + 1, :])

    def step(lanes):
        here = tile[TW : TW + CPD, lanes]
        return here + kappa_edge * ((tile[2 * TW : 2 * TW + CPD, lanes] + tile[0:CPD, lanes]) - 2.0 * here)

    used = step(slice(0, 2 * L))
    moved[:, 0 : 2 * L] = used
    both = jnp.dot(picks, split(used), preferred_element_type=jnp.float32)
    send[...] = (both[:, 0 : 2 * L] + both[:, 2 * L :]).reshape(N, 2, 2 * L)
    pl.semaphore_wait(ready, NX * NC - 1)

    def far(i):
        return (1 - 2 * lax.rem(i, 2)) * ((i + 1) // 2)

    def forward(i, carry):
        ring, plane = i // (NX * NC), lax.rem(i, NX * NC)
        peer = index_of(
            around(x + NX // 2 + far(plane // NC), NX),
            around(z + NZ // 2 + far(ring), NZ),
            lax.rem(core + 1 - lax.rem(plane, NC), NC),
        )
        pltpu.make_async_remote_copy(
            send.at[peer], recv.at[me], fwd_send, fwd_recv.at[x // 2], device_id=(peer, strip), device_id_type=MESH
        ).start()
        return carry

    lax.fori_loop(0, N - 1, forward, 0)
    pltpu.make_async_copy(send.at[me], recv.at[me], fwd_recv.at[x // 2]).start()

    moved[:, 2 * L :] = step(slice(2 * L, FL))
    rest = pltpu.make_async_copy(moved.at[:, pl.ds(2 * L, FL - 2 * L)], new_hbm.at[0, :, pl.ds(2 * L, FL - 2 * L)], store_sem.at[0])
    rest.start()

    for half in range(2):
        lanes = slice(half * HALF, (half + 1) * HALF)
        base = half * HROWS
        levels = slice(half * ZROWS, half * ZROWS + CZ)
        arrived = recv.at[pl.ds(half * N // 2, N // 2)]
        pltpu.make_async_copy(arrived, arrived, fwd_recv.at[half]).wait()
        columns = recv[half * N // 2 : (half + 1) * N // 2].reshape(HALF, 2 * L)
        both = lax.dot_general(
            weights[...], columns, (((1,), (1,)), ((), ())), precision=HIGHEST, preferred_element_type=jnp.float32
        )
        forcing = both[0:CZ]
        courant = max_courant * jax.nn.sigmoid(both[L : L + CZ])
        keep = 1.0 - courant
        nudge = relax_rate * (forcing - mean[levels, :])
        a1[0:CZ, :] = keep * rl[levels, :]
        b1[0:CZ, :] = courant * rl[levels, :]
        d1[0:CZ, :] = nudge * rl[levels, :]
        a2[0:CZ, :] = keep * ru[levels, :]
        b2[0:CZ, :] = courant * ru[levels, :]

        def row(ref, level, first=0):
            return ref[pl.ds(first + level, 1), :]

        def behind(values):
            last = pltpu.roll(values[CX - 8 : CX], 1, 0)
            return jnp.concatenate([last, values[0 : CX - 8]], axis=0)

        def up_sweep(level, carry):
            spot = pl.ds(pl.multiple_of(base + level * CX, 8), CX)
            values = field[spot, :]
            carry = (
                values * row(a1, level)
                + behind(values) * row(b1, level)
                + (row(d1, level) + row(cl, level, half * ZROWS) * carry)
            )
            field[spot, :] = carry
            return carry

        def down_sweep(i, carry):
            level = CZ - 1 - i
            solved, partial = carry
            spot = pl.ds(pl.multiple_of(base + level * CX, 8), CX)
            solved = field[spot, :] + row(el, level, half * ZROWS) * solved
            partial = solved * row(a2, level) + behind(solved) * row(b2, level) + row(cu, level, half * ZROWS) * partial
            field[spot, :] = partial
            return solved, partial

        def last_sweep(level, carry):
            spot = pl.ds(pl.multiple_of(base + level * CX, 8), CX)
            carry = field[spot, :] + row(eu, level, half * ZROWS) * carry
            field[spot, :] = carry
            eight = carry.reshape(8, 8, HALF)
            here = pl.ds(pl.multiple_of(level * 8, 8), 8)
            part[here, :] = jnp.sum(eight, axis=0)
            partsq[here, :] = jnp.sum(eight * eight, axis=0)
            return carry

        none = jnp.zeros((CX, HALF), jnp.float32)
        lax.fori_loop(0, CZ, up_sweep, none)
        lax.fori_loop(0, CZ, down_sweep, (none, none))
        lax.fori_loop(0, CZ, last_sweep, none)

        def level_sums(ref):
            blocks = []
            for block in range(ZROWS // 8):
                rows = min(8, CZ - 8 * block)
                total = ref[pl.ds(block * 64, rows, stride=8), :]
                for s in range(1, 8):
                    total = total + ref[pl.ds(block * 64 + s, rows, stride=8), :]
                blocks.append(total)
            return jnp.concatenate(blocks, axis=0) * (1.0 / CX)

        mean_after = level_sums(part)
        spread_after = level_sums(partsq) - mean_after * mean_after
        delta[0:CZ, lanes] = mean_after - mean[levels, :]
        delta[L : L + CZ, lanes] = spread_after - spread[levels, :]
        tend = lax.dot_general(
            delta[:, lanes], weights[...], (((0,), (0,)), ((), ())), precision=HIGHEST, preferred_element_type=jnp.float32
        )
        reply[half * N // 2 : (half + 1) * N // 2] = tend.reshape(N // 2, 2, 2 * L)

        def back(i, carry):
            ring, plane = i // 4, lax.rem(i, 4)
            peer = index_of(
                2 * half + lax.rem(x + plane // NC + 1, 2),
                around(z + NZ // 2 + far(ring), NZ),
                lax.rem(core + 1 - lax.rem(plane, NC), NC),
            )

            @pl.when(peer != me)
            def _():
                pltpu.make_async_remote_copy(
                    reply.at[peer], ret.at[me], rep_send, rep_recv, device_id=(peer, strip), device_id_type=MESH
                ).start()

            return carry

        lax.fori_loop(0, N // 2, back, 0)

        @pl.when(x // 2 == half)
        def _():
            pltpu.make_async_copy(reply.at[me], ret.at[me], rep_recv).start()

    def store(column, carry):
        spot = lax.rem(column, 8) * 8 + column // 8
        for half in range(2):
            blocks = []
            for block in range(ZROWS // 8):
                rows = min(8, CZ - 8 * block)
                blocks.append(field[pl.ds(half * HROWS + block * 8 * CX + spot, rows, stride=CX), :])
            start = pl.multiple_of(column * SLOTS + half * HALF, HALF)
            crm[:, pl.ds(start, HALF)] = jnp.concatenate(blocks, axis=0).astype(jnp.bfloat16)
        return carry

    crm_stores = []
    for i in range(pieces):
        lax.fori_loop(i * CX // pieces, (i + 1) * CX // pieces, store, 0)
        crm_stores.append(
            pltpu.make_async_copy(
                crm.at[:, pl.ds(i * width, width)], out_hbm.at[0, 0, :, pl.ds(i * width, width)], crm_out_sem.at[i]
            )
        )
        crm_stores[-1].start()

    pltpu.make_async_copy(ret, ret, rep_recv).wait()
    both = lax.dot_general(
        picks, split(ret[...].reshape(SLOTS, 2 * L)), (((0,), (0,)), ((), ())), preferred_element_type=jnp.float32
    )
    moved[:, 0 : 2 * L] = moved[:, 0 : 2 * L] + (both[:, 0 : 2 * L] + both[:, 2 * L :])
    first = pltpu.make_async_copy(moved.at[:, pl.ds(0, 2 * L)], new_hbm.at[0, :, pl.ds(0, 2 * L)], store_sem.at[1])
    first.start()
    sent = send.at[pl.ds(0, N - 1)]
    pltpu.make_async_copy(sent, sent, fwd_send).wait()
    pltpu.make_async_copy(sent, sent, rep_send).wait()
    for piece in crm_stores:
        piece.wait()
    rest.wait()
    first.wait()


def shards(state, owners, orient, crm_state, active_levels, vertical_map, diffusion):
    f32 = jnp.float32
    anywhere = pl.BlockSpec(memory_space=pl.ANY)
    level_rows = pltpu.VMEM((2 * ZROWS, HALF), f32)
    half_rows = pltpu.VMEM((ZROWS, HALF), f32)
    chunks = pltpu.VMEM((N, 2, 2 * L), f32)
    dma = pltpu.SemaphoreType.DMA
    return pl.pallas_call(
        kernel,
        out_shape=(
            jax.ShapeDtypeStruct(state.shape, f32),
            jax.ShapeDtypeStruct(crm_state.shape, jnp.bfloat16),
        ),
        in_specs=[anywhere] * 7,
        out_specs=(anywhere, anywhere),
        scratch_shapes=[
            pltpu.VMEM((2 * TW + CPD, FL), f32),
            pltpu.VMEM((2, TW, FL), f32),
            pltpu.VMEM((1, CPD), jnp.int32),
            pltpu.VMEM((1, SLOTS), jnp.int32),
            pltpu.VMEM((CZ, L), f32),
            pltpu.SMEM((1, 2), jnp.int32),
            pltpu.SMEM((1, CZ - 1), f32),
            pltpu.VMEM((CZ, CX * SLOTS), jnp.bfloat16),
            pltpu.VMEM((2 * HROWS, HALF), f32),
            *[level_rows] * 6,
            *[half_rows] * 5,
            *[level_rows] * 2,
            pltpu.VMEM((ZROWS * 8, HALF), f32),
            pltpu.VMEM((ZROWS * 8, HALF), f32),
            pltpu.VMEM((CPD, CPD), f32),
            pltpu.VMEM((CPD, SLOTS), f32),
            pltpu.VMEM((CPD, FL), f32),
            chunks,
            chunks,
            chunks,
            chunks,
            pltpu.SemaphoreType.REGULAR,
            dma((6,)),
            dma((4,)),
            dma((2,)),
            dma((2,)),
            dma,
            dma((2,)),
            dma,
            dma,
            dma((2,)),
            dma((4,)),
        ],
        compiler_params=pltpu.CompilerParams(collective_id=0, has_side_effects=True, vmem_limit_bytes=48 << 20),
    )(
        state,
        owners.reshape(1, CPD),
        orient.reshape(1, 2),
        crm_state,
        active_levels.reshape(1, SLOTS),
        vertical_map,
        diffusion.reshape(1, CZ - 1),
    )


def solution(mesh):
    in_specs = (
        P("edge", "cols", None),
        P("edge", "cols", None),
        P("edge", "cols", None),
        P("edge", "cols", None, None),
        P("edge", "cols", None),
        P(),
        P(),
    )
    out_specs = (P("edge", "cols", None), P("edge", "cols", None, None))
    return jax.shard_map(shards, mesh=mesh, in_specs=in_specs, out_specs=out_specs, check_vma=False)
```

time: 143 us -> 55.9 us (0.39)
  Pallas kernels: 0 us -> 46.4 us
  starting transfers between devices: 36.7 us -> 0 us
  local copies, waits for them, and re-layouts: 43.8 us -> 7.96 us
  other arithmetic: 29.3 us -> 0 us
  waiting for transfers between devices: 26.3 us -> 0 us
  between operations: 3.69 us -> 0.66 us
    pallas_call x0 -> x1, Pallas kernels: none -> 46.4 us  [shards(): pl.pallas_call(kernel, out_shape=(jax.ShapeDtypeStruct(state.shape, f32),...]
    another operation x60 -> x0, local copies, waits for them, and re-layouts: 32.4 us -> none  [tridiag(): return jnp.stack(solved, axis=0)]
    all_to_all x2 -> x0, starting transfers between devices: 30.1 us -> none  [the longest x1 20.7 us: shards(): lax.all_to_all(outgoing, 'cols', split_axis=0, concat_axis=0, tiled=True)]
    all_to_all x2 -> x0, waiting for transfers between devices: 26.3 us -> none  [the longest x1 26.3 us: shards(): lax.all_to_all(outgoing, 'cols', split_axis=0, concat_axis=0, tiled=True)]
    another operation x59 -> x0, other arithmetic: 10.2 us -> none
    ppermute x2 -> x0, starting transfers between devices: 6.55 us -> none  [from_behind(): return lax.ppermute(value, axis, pairs)]
    reduce_sum x3 -> x0, other arithmetic: 5.55 us -> none  [the longest x1 3.24 us: physics(): mean_before = jnp.mean(field, axis=1)]
    unnamed x92 -> x16, local copies, waits for them, and re-layouts: 4.46 us -> 7.96 us
  transfers between devices with their start and end apart: 4 -> 0, of which waited for: 1 -> 0; matrix products, arithmetic and copies ran while one was open for 32% -> 0% of each run, Pallas kernels for 0% -> 0%
where the time goes in v1:
time: 55.9 us; the launch traced here: 55 us
  Pallas kernels  46.4 us (83%)
  local copies, waits for them, and re-layouts  7.96 us (14%)
  between operations  0.66 us (1%)
    pallas_call x1, Pallas kernels, shards(): pl.pallas_call(kernel, out_shape=(jax.ShapeDtypeStruct(state.shape, f32),...  46.4 us
    unnamed x16, local copies, waits for them, and re-layouts  7.96 us

profile of v1, /device:TPU:7, one launch (start us, length us, event | category | flops | bytes accessed | tf_op | source)
XLA Modules:
  0.0 55.0 jit_solution(16871621920844440464)
XLA Ops:
  0.6 0.0 copy-start
  0.6 1.6 %copy-done = bf16[1,1,58,16384]{3,2,1,0:T(8,128)(2,1)S(1)} copy-done((bf16[1,1,58,16384]{3,2,1,0:T(8,128)(2,1)S(1)}, bf16[1,1,58,16384]{3,2,1,0:T(8,128)(2,1)}, u32[]{:S(2)}) %copy-start) | copy-done | bytes 1900568
  2.2 0.0 copy-start.1
  2.2 0.9 %copy-done.1 = f32[1,128,512]{2,1,0:T(8,128)S(1)} copy-done((f32[1,128,512]{2,1,0:T(8,128)S(1)}, f32[1,128,512]{2,1,0:T(8,128)}, u32[]{:S(2)}) %copy-start.1) | copy-done | bytes 262168
  3.2 0.0 copy-start.2
  3.2 0.8 %copy-done.2 = f32[58,64]{1,0:T(8,128)S(1)} copy-done((f32[58,64]{1,0:T(8,128)S(1)}, f32[58,64]{1,0:T(8,128)}, u32[]{:S(2)}) %copy-start.2) | copy-done | bytes 14872
  3.9 0.0 copy-start.3
  3.9 0.7 %copy-done.3 = s32[1,1,256]{2,1,0:T(1,128)S(1)} copy-done((s32[1,1,256]{2,1,0:T(1,128)S(1)}, s32[1,1,256]{2,1,0:T(1,128)}, u32[]{:S(2)}) %copy-start.3) | copy-done | bytes 1048
  4.6 0.0 copy-start.4
  4.6 0.7 %copy-done.4 = s32[1,128,1]{1,2,0:T(1,128)S(1)} copy-done((s32[1,128,1]{1,2,0:T(1,128)S(1)}, s32[1,128,1]{1,2,0:T(1,128)}, u32[]{:S(2)}) %copy-start.4) | copy-done | bytes 536
  5.3 0.0 copy-start.5
  5.3 0.7 %copy-done.5 = s32[1,1,2]{2,1,0:T(1,128)S(1)} copy-done((s32[1,1,2]{2,1,0:T(1,128)S(1)}, s32[1,1,2]{2,1,0:T(1,128)}, u32[]{:S(2)}) %copy-start.5) | copy-done | bytes 32
  5.9 0.0 copy-start.6
  5.9 0.7 %copy-done.6 = f32[57]{0:T(128)S(1)} copy-done((f32[57]{0:T(128)S(1)}, f32[57]{0:T(128)}, u32[]{:S(2)}) %copy-start.6) | copy-done | bytes 252
  6.6 46.4 %shard_map.86 = (f32[1,128,512]{2,1,0:T(8,128)S(1)}, bf16[1,1,58,16384]{3,2,1,0:T(8,128)(2,1)S(1)}) custom-call(f32[1,128,512]{2,1,0:T(8,128)S(1)} %copy-done.1, s32[1,128]{1,0:T(1,128)S(1)} %bitcast.5, s32[1,2]{1,0:T(1,128)S(1)} %bitcast.6, bf16[1,1,58,16384]{3,2,1,0:T(8,128)(2,1)S(1)} %copy-done, s32[1,256]{1,0:T(1,128)S(1)} %bitcast.4, ...), custom_call_target="tpu_custom_call" | custom-call | tf_op jit(solution)/shard_map/pallas_call | solution.py:379
  52.9 0.7 %copy.11 = f32[1,128,512]{2,1,0:T(8,128)} copy(f32[1,128,512]{2,1,0:T(8,128)S(1)} %get-tuple-element.4) | data formatting | bytes 524288
  53.6 1.3 %copy.12 = bf16[1,1,58,16384]{3,2,1,0:T(8,128)(2,1)} copy(bf16[1,1,58,16384]{3,2,1,0:T(8,128)(2,1)S(1)} %get-tuple-element.5) | data formatting | bytes 3801088
Async XLA Ops:
  0.6 1.6 %copy-start = (bf16[1,1,58,16384]{3,2,1,0:T(8,128)(2,1)S(1)}, bf16[1,1,58,16384]{3,2,1,0:T(8,128)(2,1)}, u32[]{:S(2)}) copy-start(bf16[1,1,58,16384]{3,2,1,0:T(8,128)(2,1)} %crm_hbm.1) | copy-start | bytes 5701636
  2.2 0.9 %copy-start.1 = (f32[1,128,512]{2,1,0:T(8,128)S(1)}, f32[1,128,512]{2,1,0:T(8,128)}, u32[]{:S(2)}) copy-start(f32[1,128,512]{2,1,0:T(8,128)} %state_hbm.1) | copy-start | bytes 786436
  3.2 0.8 %copy-start.2 = (f32[58,64]{1,0:T(8,128)S(1)}, f32[58,64]{1,0:T(8,128)}, u32[]{:S(2)}) copy-start(f32[58,64]{1,0:T(8,128)} %vmap_hbm.1) | copy-start | bytes 44548
  3.9 0.7 %copy-start.3 = (s32[1,1,256]{2,1,0:T(1,128)S(1)}, s32[1,1,256]{2,1,0:T(1,128)}, u32[]{:S(2)}) copy-start(s32[1,1,256]{2,1,0:T(1,128)} %param.11) | copy-start | bytes 3076
  4.6 0.7 %copy-start.4 = (s32[1,128,1]{1,2,0:T(1,128)S(1)}, s32[1,128,1]{1,2,0:T(1,128)}, u32[]{:S(2)}) copy-start(s32[1,128,1]{1,2,0:T(1,128)} %param.8) | copy-start | bytes 1540
  5.3 0.7 %copy-start.5 = (s32[1,1,2]{2,1,0:T(1,128)S(1)}, s32[1,1,2]{2,1,0:T(1,128)}, u32[]{:S(2)}) copy-start(s32[1,1,2]{2,1,0:T(1,128)} %param.9) | copy-start | bytes 28
  5.9 0.7 %copy-start.6 = (f32[57]{0:T(128)S(1)}, f32[57]{0:T(128)}, u32[]{:S(2)}) copy-start(f32[57]{0:T(128)} %param.13) | copy-start | bytes 688

commit v2 on v1

--- a/solution.py
+++ b/solution.py
@@ -45,11 +45,11 @@
 
 def kernel(
     state_hbm, owners_hbm, orient_hbm, crm_hbm, active_hbm, vmap_hbm, diff_hbm,
-    new_hbm, out_hbm,
+    new, out,
     tile, ghosts, owner, active, vmap, orient, diff, crm, field,
     rl, cl, el, ru, cu, eu, a1, b1, d1, a2, b2, mean, spread, part, partsq,
-    weights, delta, moved, send, recv, reply, ret,
-    ready, load_sem, crm_sem, halo_send, halo_recv, fwd_send, fwd_recv, rep_send, rep_recv, store_sem, crm_out_sem,
+    weights, delta, send, recv, reply, ret,
+    ready, load_sem, crm_sem, halo_send, halo_recv, fwd_send, fwd_recv, rep_send, rep_recv,
 ):
     me = lax.axis_index("cols")
     strip = lax.axis_index("edge")
@@ -104,6 +104,81 @@
     for load in loads:
         load.wait()
 
+    group = owner[...]
+    line = lax.broadcasted_iota(jnp.int32, (CPD, CPD), 0)
+    along = lax.broadcasted_iota(jnp.int32, (CPD, CPD), 1)
+    named = jnp.where(line == group, 1.0, 0.0)
+    earlier = jnp.where(line < along, 1.0, 0.0)
+    before = jnp.dot(named.astype(jnp.bfloat16), earlier.astype(jnp.bfloat16), preferred_element_type=jnp.float32)
+    rank = jnp.sum(named * before, axis=0, keepdims=True)
+    slot = group * 2 + rank.astype(jnp.int32)
+    picks = jnp.where(lax.broadcasted_iota(jnp.int32, (SLOTS, CPD), 0) == slot, 1.0, 0.0).astype(jnp.bfloat16)
+
+    pl.semaphore_wait(barrier, NZ - 1 + NX * NC - 1 + 2)
+
+    def announce(i, carry):
+        pl.semaphore_signal(ready, inc=1, device_id=(plane_peer(i), strip), device_id_type=MESH)
+        return carry
+
+    upward = pltpu.make_async_remote_copy(
+        state_hbm.at[0, pl.ds(CPD - TW, TW)], ghosts.at[0], halo_send.at[0], halo_recv.at[0],
+        device_id=(me, above), device_id_type=MESH,
+    )
+    downward = pltpu.make_async_remote_copy(
+        state_hbm.at[0, pl.ds(0, TW)], ghosts.at[1], halo_send.at[1], halo_recv.at[1],
+        device_id=(me, below), device_id_type=MESH,
+    )
+    upward.start()
+    downward.start()
+    lax.fori_loop(1, NX * NC, announce, 0)
+    upward.wait()
+    downward.wait()
+    for side in range(2):
+        flip = orient[0, side] == 1
+        for w in range(TW):
+            row = side * (TW + CPD) + w
+            tile[row : row + 1, :] = jnp.where(flip, ghosts[side, TW - 1 - w : TW - w, :], ghosts[side, w : w + 1, :])
+
+    def step(lanes):
+        here = tile[TW : TW + CPD, lanes]
+        return here + kappa_edge * ((tile[2 * TW : 2 * TW + CPD, lanes] + tile[0:CPD, lanes]) - 2.0 * here)
+
+    used = step(slice(0, 2 * L))
+    new[0, :, 0 : 2 * L] = used
+    both = jnp.dot(picks, split(used), preferred_element_type=jnp.float32)
+    send[...] = (both[:, 0 : 2 * L] + both[:, 2 * L :]).reshape(N, 2, 2 * L)
+    pl.semaphore_wait(ready, NX * NC - 1)
+
+    far = z + NZ // 2
+
+    def rings(send_ring):
+        send_ring(lax.rem(far, NZ))
+
+        def pair(i, carry):
+            send_ring(lax.rem(far + i, NZ))
+            send_ring(lax.rem(far - i, NZ))
+            return carry
+
+        lax.fori_loop(1, NZ // 2, pair, 0)
+
+    others = [
+        (lax.rem(x + dx, NX) * (NZ * NC) + lax.rem(core + dc, NC)) for dx in (2, 1, 3, 0) for dc in (1, 0)
+    ]
+    arrival = fwd_recv.at[lax.div(x, 2)]
+
+    def forward(peers, level):
+        for plane in peers:
+            peer = plane + level * NC
+            pltpu.make_async_remote_copy(
+                send.at[peer], recv.at[me], fwd_send, arrival, device_id=(peer, strip), device_id_type=MESH
+            ).start()
+
+    rings(functools.partial(forward, others))
+    forward(others[:-1], z)
+    pltpu.make_async_copy(send.at[me], recv.at[me], arrival).start()
+
+    new[0, :, 2 * L :] = step(slice(2 * L, FL))
+
     count = active[...]
 
     def put(ref, level, values):
@@ -162,73 +237,6 @@
         mean[levels, :] = average
         spread[levels, :] = sums[2 + half] * (1.0 / CX) - average * average
 
-    group = owner[...]
-    line = lax.broadcasted_iota(jnp.int32, (CPD, CPD), 0)
-    along = lax.broadcasted_iota(jnp.int32, (CPD, CPD), 1)
-    named = jnp.where(line == group, 1.0, 0.0)
-    earlier = jnp.where(line < along, 1.0, 0.0)
-    before = jnp.dot(named.astype(jnp.bfloat16), earlier.astype(jnp.bfloat16), preferred_element_type=jnp.float32)
-    rank = jnp.sum(named * before, axis=0, keepdims=True)
-    slot = group * 2 + rank.astype(jnp.int32)
-    picks = jnp.where(lax.broadcasted_iota(jnp.int32, (SLOTS, CPD), 0) == slot, 1.0, 0.0).astype(jnp.bfloat16)
-
-    pl.semaphore_wait(barrier, NZ - 1 + NX * NC - 1 + 2)
-
-    def announce(i, carry):
-        pl.semaphore_signal(ready, inc=1, device_id=(plane_peer(i), strip), device_id_type=MESH)
-        return carry
-
-    upward = pltpu.make_async_remote_copy(
-        state_hbm.at[0, pl.ds(CPD - TW, TW)], ghosts.at[0], halo_send.at[0], halo_recv.at[0],
-        device_id=(me, above), device_id_type=MESH,
-    )
-    downward = pltpu.make_async_remote_copy(
-        state_hbm.at[0, pl.ds(0, TW)], ghosts.at[1], halo_send.at[1], halo_recv.at[1],
-        device_id=(me, below), device_id_type=MESH,
-    )
-    upward.start()
-    downward.start()
-    lax.fori_loop(1, NX * NC, announce, 0)
-    upward.wait()
-    downward.wait()
-    for side in range(2):
-        flip = orient[0, side] == 1
-        for w in range(TW):
-            row = side * (TW + CPD) + w
-            tile[row : row + 1, :] = jnp.where(flip, ghosts[side, TW - 1 - w : TW - w, :], ghosts[side, w : w + 1, :])
-
-    def step(lanes):
-        here = tile[TW : TW + CPD, lanes]
-        return here + kappa_edge * ((tile[2 * TW : 2 * TW + CPD, lanes] + tile[0:CPD, lanes]) - 2.0 * here)
-
-    used = step(slice(0, 2 * L))
-    moved[:, 0 : 2 * L] = used
-    both = jnp.dot(picks, split(used), preferred_element_type=jnp.float32)
-    send[...] = (both[:, 0 : 2 * L] + both[:, 2 * L :]).reshape(N, 2, 2 * L)
-    pl.semaphore_wait(ready, NX * NC - 1)
-
-    def far(i):
-        return (1 - 2 * lax.rem(i, 2)) * ((i + 1) // 2)
-
-    def forward(i, carry):
-        ring, plane = i // (NX * NC), lax.rem(i, NX * NC)
-        peer = index_of(
-            around(x + NX // 2 + far(plane // NC), NX),
-            around(z + NZ // 2 + far(ring), NZ),
-            lax.rem(core + 1 - lax.rem(plane, NC), NC),
-        )
-        pltpu.make_async_remote_copy(
-            send.at[peer], recv.at[me], fwd_send, fwd_recv.at[x // 2], device_id=(peer, strip), device_id_type=MESH
-        ).start()
-        return carry
-
-    lax.fori_loop(0, N - 1, forward, 0)
-    pltpu.make_async_copy(send.at[me], recv.at[me], fwd_recv.at[x // 2]).start()
-
-    moved[:, 2 * L :] = step(slice(2 * L, FL))
-    rest = pltpu.make_async_copy(moved.at[:, pl.ds(2 * L, FL - 2 * L)], new_hbm.at[0, :, pl.ds(2 * L, FL - 2 * L)], store_sem.at[0])
-    rest.start()
-
     for half in range(2):
         lanes = slice(half * HALF, (half + 1) * HALF)
         base = half * HROWS
@@ -310,23 +318,21 @@
         )
         reply[half * N // 2 : (half + 1) * N // 2] = tend.reshape(N // 2, 2, 2 * L)
 
-        def back(i, carry):
-            ring, plane = i // 4, lax.rem(i, 4)
-            peer = index_of(
-                2 * half + lax.rem(x + plane // NC + 1, 2),
-                around(z + NZ // 2 + far(ring), NZ),
-                lax.rem(core + 1 - lax.rem(plane, NC), NC),
-            )
-
-            @pl.when(peer != me)
-            def _():
+        targets = [xt * (NZ * NC) + ct for xt in (2 * half, 2 * half + 1) for ct in range(NC)]
+
+        def back(peers, level):
+            for plane in peers:
+                peer = plane + level * NC
                 pltpu.make_async_remote_copy(
                     reply.at[peer], ret.at[me], rep_send, rep_recv, device_id=(peer, strip), device_id_type=MESH
                 ).start()
 
-            return carry
-
-        lax.fori_loop(0, N // 2, back, 0)
+        rings(functools.partial(back, targets))
+        for plane in targets:
+
+            @pl.when(plane + z * NC != me)
+            def _(plane=plane):
+                back([plane], z)
 
         @pl.when(x // 2 == half)
         def _():
@@ -340,33 +346,31 @@
                 rows = min(8, CZ - 8 * block)
                 blocks.append(field[pl.ds(half * HROWS + block * 8 * CX + spot, rows, stride=CX), :])
             start = pl.multiple_of(column * SLOTS + half * HALF, HALF)
-            crm[:, pl.ds(start, HALF)] = jnp.concatenate(blocks, axis=0).astype(jnp.bfloat16)
+            out[0, 0, :, pl.ds(start, HALF)] = jnp.concatenate(blocks, axis=0).astype(jnp.bfloat16)
         return carry
 
-    crm_stores = []
-    for i in range(pieces):
-        lax.fori_loop(i * CX // pieces, (i + 1) * CX // pieces, store, 0)
-        crm_stores.append(
-            pltpu.make_async_copy(
-                crm.at[:, pl.ds(i * width, width)], out_hbm.at[0, 0, :, pl.ds(i * width, width)], crm_out_sem.at[i]
-            )
-        )
-        crm_stores[-1].start()
+    lax.fori_loop(0, CX, store, 0)
 
     pltpu.make_async_copy(ret, ret, rep_recv).wait()
     both = lax.dot_general(
         picks, split(ret[...].reshape(SLOTS, 2 * L)), (((0,), (0,)), ((), ())), preferred_element_type=jnp.float32
     )
-    moved[:, 0 : 2 * L] = moved[:, 0 : 2 * L] + (both[:, 0 : 2 * L] + both[:, 2 * L :])
-    first = pltpu.make_async_copy(moved.at[:, pl.ds(0, 2 * L)], new_hbm.at[0, :, pl.ds(0, 2 * L)], store_sem.at[1])
-    first.start()
+    new[0, :, 0 : 2 * L] = new[0, :, 0 : 2 * L] + (both[:, 0 : 2 * L] + both[:, 2 * L :])
     sent = send.at[pl.ds(0, N - 1)]
     pltpu.make_async_copy(sent, sent, fwd_send).wait()
     pltpu.make_async_copy(sent, sent, rep_send).wait()
-    for piece in crm_stores:
-        piece.wait()
-    rest.wait()
-    first.wait()
+
+def ship(new, out, new_hbm, out_hbm, sems):
+    pieces = 8
+    width = CX * SLOTS // pieces
+    copies = [pltpu.make_async_copy(new, new_hbm, sems.at[pieces])]
+    for i in range(pieces):
+        lanes = pl.ds(i * width, width)
+        copies.append(pltpu.make_async_copy(out.at[0, 0, :, lanes], out_hbm.at[0, 0, :, lanes], sems.at[i]))
+    for copy in copies:
+        copy.start()
+    for copy in copies:
+        copy.wait()
 
 
 def shards(state, owners, orient, crm_state, active_levels, vertical_map, diffusion):
@@ -376,14 +380,14 @@
     half_rows = pltpu.VMEM((ZROWS, HALF), f32)
     chunks = pltpu.VMEM((N, 2, 2 * L), f32)
     dma = pltpu.SemaphoreType.DMA
-    return pl.pallas_call(
+    new, out = pl.pallas_call(
         kernel,
         out_shape=(
-            jax.ShapeDtypeStruct(state.shape, f32),
-            jax.ShapeDtypeStruct(crm_state.shape, jnp.bfloat16),
+            pltpu.VMEM(state.shape, f32),
+            pltpu.VMEM(crm_state.shape, jnp.bfloat16),
         ),
         in_specs=[anywhere] * 7,
-        out_specs=(anywhere, anywhere),
+        out_specs=(pl.BlockSpec(memory_space=pltpu.VMEM),) * 2,
         scratch_shapes=[
             pltpu.VMEM((2 * TW + CPD, FL), f32),
             pltpu.VMEM((2, TW, FL), f32),
@@ -401,7 +405,6 @@
             pltpu.VMEM((ZROWS * 8, HALF), f32),
             pltpu.VMEM((CPD, CPD), f32),
             pltpu.VMEM((CPD, SLOTS), f32),
-            pltpu.VMEM((CPD, FL), f32),
             chunks,
             chunks,
             chunks,
@@ -415,10 +418,8 @@
             dma((2,)),
             dma,
             dma,
-            dma((2,)),
-            dma((4,)),
         ],
-        compiler_params=pltpu.CompilerParams(collective_id=0, has_side_effects=True, vmem_limit_bytes=48 << 20),
+        compiler_params=pltpu.CompilerParams(collective_id=0, has_side_effects=True, vmem_limit_bytes=56 << 20),
     )(
         state,
         owners.reshape(1, CPD),
@@ -428,6 +429,17 @@
         vertical_map,
         diffusion.reshape(1, CZ - 1),
     )
+    return pl.pallas_call(
+        ship,
+        out_shape=(
+            pltpu.HBM(state.shape, f32),
+            pltpu.HBM(crm_state.shape, jnp.bfloat16),
+        ),
+        in_specs=[anywhere] * 2,
+        out_specs=(pl.BlockSpec(memory_space=pltpu.HBM),) * 2,
+        scratch_shapes=[dma((9,))],
+        compiler_params=pltpu.CompilerParams(vmem_limit_bytes=8 << 20),
+    )(new, out)
 
 
 def solution(mesh):

time: 55.9 us -> 45.6 us (0.82); the launches traced: 55 us -> 45.3 us
  local copies, waits for them, and re-layouts: 7.96 us -> 0 us
  Pallas kernels: 46.4 us -> 44.7 us
    unnamed x16 -> x0, local copies, waits for them, and re-layouts: 7.96 us -> none
    pallas_call x1 -> x2, Pallas kernels: 46.4 us -> 44.7 us  [the longest x1 43.2 us: shards(): pl.pallas_call(kernel, out_shape=(pltpu.VMEM(state.shape, f32), pltpu.VME...]
where the time goes in v2:
time: 45.6 us; the launch traced here: 45.3 us
  Pallas kernels  44.7 us (98%)
  between operations  0.64 us (1%)
    pallas_call x1, Pallas kernels, shards(): pl.pallas_call(kernel, out_shape=(pltpu.VMEM(state.shape, f32), pltpu.VME...  43.2 us
    pallas_call x1, Pallas kernels, shards(): pl.pallas_call(ship, out_shape=(pltpu.HBM(state.shape, f32), pltpu.HBM(cr...  1.47 us

profile of v2, /device:TPU:7, one launch (start us, length us, event | category | flops | bytes accessed | tf_op | source)
XLA Modules:
  0.0 45.3 jit_solution(15996908847130173171)
XLA Ops:
  0.6 43.2 %shard_map.86 = (f32[1,128,512]{2,1,0:T(8,128)S(1)}, bf16[1,1,58,16384]{3,2,1,0:T(8,128)(2,1)S(1)}) custom-call(f32[1,128,512]{2,1,0:T(8,128)} %state_hbm.1, s32[1,128]{1,0:T(1,128)} %bitcast.5, s32[1,2]{1,0:T(1,128)} %bitcast.6, bf16[1,1,58,16384]{3,2,1,0:T(8,128)(2,1)} %crm_hbm.1, s32[1,256]{1,0:T(1,128)} %bitcast.4, f32[58,64]{1,0:T(8,128)} %vmap_hbm.1, ...), custom_call_target="tpu_custom_call" | custom-call | tf_op jit(solution)/shard_map/pallas_call | solution.py:383
  43.8 1.5 %shard_map.87 = (f32[1,128,512]{2,1,0:T(8,128)}, bf16[1,1,58,16384]{3,2,1,0:T(8,128)(2,1)}) custom-call(f32[1,128,512]{2,1,0:T(8,128)S(1)} %get-tuple-element.4.new, bf16[1,1,58,16384]{3,2,1,0:T(8,128)(2,1)S(1)} %get-tuple-element.5.out), custom_call_target="tpu_custom_call" | custom-call | tf_op jit(solution)/shard_map/pallas_call | solution.py:432

commit v3 on v2

--- a/solution.py
+++ b/solution.py
@@ -26,7 +26,7 @@
 max_courant = 0.9
 relax_rate = 0.5
 
-HIGHEST = lax.Precision.HIGHEST
+UNROLL = 29
 
 
 def index_of(x, z, core):
@@ -41,6 +41,19 @@
     high = values.astype(jnp.bfloat16)
     low = (values - high.astype(jnp.float32)).astype(jnp.bfloat16)
     return jnp.concatenate([high, low], axis=1)
+
+
+def product(left, right, left_dim, right_dim):
+    def parts(values):
+        high = values.astype(jnp.bfloat16)
+        return high, (values - high.astype(jnp.float32)).astype(jnp.bfloat16)
+
+    def dot(a, b):
+        return lax.dot_general(a, b, (((left_dim,), (right_dim,)), ((), ())), preferred_element_type=jnp.float32)
+
+    left_high, left_low = parts(left)
+    right_high, right_low = parts(right)
+    return dot(left_high, right_high) + (dot(left_high, right_low) + dot(left_low, right_high))
 
 
 def kernel(
@@ -64,20 +77,25 @@
     def greet(column, row):
         pl.semaphore_signal(barrier, inc=1, device_id=(column, row), device_id_type=MESH)
 
-    def greet_ring(i, carry):
-        greet(index_of(x, around(z + i, NZ), core), strip)
+    far = z + NZ // 2
+
+    def ring(level):
+        greet(index_of(x, lax.rem(level, NZ), core), strip)
+
+    ring(far)
+
+    def greet_pair(i, carry):
+        ring(far - i)
+        ring(far + i)
         return carry
 
-    def plane_peer(i):
-        i = i + core + NC * x
-        return index_of(lax.rem(i // NC, NX), z, lax.rem(i, NC))
-
-    def greet_plane(i, carry):
-        greet(plane_peer(i), strip)
-        return carry
-
-    lax.fori_loop(1, NZ, greet_ring, 0)
-    lax.fori_loop(1, NX * NC, greet_plane, 0)
+    lax.fori_loop(1, NZ // 2, greet_pair, 0)
+
+    planes = [
+        (lax.rem(x + dx, NX) * (NZ * NC) + lax.rem(core + dc, NC)) for dx in (2, 1, 3, 0) for dc in (1, 0)
+    ]
+    for plane in planes[:-1]:
+        greet(plane + z * NC, strip)
     greet(me, above)
     greet(me, below)
 
@@ -116,28 +134,33 @@
 
     pl.semaphore_wait(barrier, NZ - 1 + NX * NC - 1 + 2)
 
-    def announce(i, carry):
-        pl.semaphore_signal(ready, inc=1, device_id=(plane_peer(i), strip), device_id_type=MESH)
-        return carry
-
-    upward = pltpu.make_async_remote_copy(
-        state_hbm.at[0, pl.ds(CPD - TW, TW)], ghosts.at[0], halo_send.at[0], halo_recv.at[0],
-        device_id=(me, above), device_id_type=MESH,
-    )
-    downward = pltpu.make_async_remote_copy(
-        state_hbm.at[0, pl.ds(0, TW)], ghosts.at[1], halo_send.at[1], halo_recv.at[1],
-        device_id=(me, below), device_id_type=MESH,
-    )
-    upward.start()
-    downward.start()
-    lax.fori_loop(1, NX * NC, announce, 0)
-    upward.wait()
-    downward.wait()
-    for side in range(2):
-        flip = orient[0, side] == 1
-        for w in range(TW):
-            row = side * (TW + CPD) + w
-            tile[row : row + 1, :] = jnp.where(flip, ghosts[side, TW - 1 - w : TW - w, :], ghosts[side, w : w + 1, :])
+    parts = (slice(0, 2 * L), slice(2 * L, FL))
+    trades = []
+    for i, lanes in enumerate(parts):
+        for side, (first, row) in enumerate(((CPD, above), (TW, below))):
+            trades.append(
+                pltpu.make_async_remote_copy(
+                    tile.at[pl.ds(first, TW), lanes], ghosts.at[side, :, lanes],
+                    halo_send.at[2 * i + side], halo_recv.at[2 * i + side],
+                    device_id=(me, row), device_id_type=MESH,
+                )
+            )
+            trades[-1].start()
+    for plane in planes[:-1]:
+        pl.semaphore_signal(ready, inc=1, device_id=(plane + z * NC, strip), device_id_type=MESH)
+
+    def settle(i):
+        lanes = parts[i]
+        for side in range(2):
+            trades[2 * i + side].wait()
+            flip = orient[0, side] == 1
+            for w in range(TW):
+                row = side * (TW + CPD) + w
+                tile[row : row + 1, lanes] = jnp.where(
+                    flip, ghosts[side, TW - 1 - w : TW - w, lanes], ghosts[side, w : w + 1, lanes]
+                )
+
+    settle(0)
 
     def step(lanes):
         here = tile[TW : TW + CPD, lanes]
@@ -149,21 +172,16 @@
     send[...] = (both[:, 0 : 2 * L] + both[:, 2 * L :]).reshape(N, 2, 2 * L)
     pl.semaphore_wait(ready, NX * NC - 1)
 
-    far = z + NZ // 2
-
     def rings(send_ring):
         send_ring(lax.rem(far, NZ))
 
         def pair(i, carry):
+            send_ring(lax.rem(far - i, NZ))
             send_ring(lax.rem(far + i, NZ))
-            send_ring(lax.rem(far - i, NZ))
             return carry
 
         lax.fori_loop(1, NZ // 2, pair, 0)
 
-    others = [
-        (lax.rem(x + dx, NX) * (NZ * NC) + lax.rem(core + dc, NC)) for dx in (2, 1, 3, 0) for dc in (1, 0)
-    ]
     arrival = fwd_recv.at[lax.div(x, 2)]
 
     def forward(peers, level):
@@ -173,10 +191,38 @@
                 send.at[peer], recv.at[me], fwd_send, arrival, device_id=(peer, strip), device_id_type=MESH
             ).start()
 
-    rings(functools.partial(forward, others))
-    forward(others[:-1], z)
-    pltpu.make_async_copy(send.at[me], recv.at[me], arrival).start()
-
+    def forward_all():
+        rings(functools.partial(forward, planes))
+        forward(planes[:-1], z)
+        pltpu.make_async_copy(send.at[me], recv.at[me], arrival).start()
+
+    forward_all()
+
+    sums = tuple(jnp.zeros((CZ, HALF), jnp.float32) for _ in range(4))
+
+    def relayout(column, carry):
+        carry = list(carry)
+        spot = lax.rem(column, 8) * 8 + column // 8
+        for half in range(2):
+            start = pl.multiple_of(column * SLOTS + half * HALF, HALF)
+            values = crm[:, pl.ds(start, HALF)].astype(jnp.float32)
+            carry[half] = carry[half] + values
+            carry[2 + half] = carry[2 + half] + values * values
+            for block in range(ZROWS // 8):
+                rows = min(8, CZ - 8 * block)
+                field[pl.ds(half * HROWS + block * 8 * CX + spot, rows, stride=CX), :] = values[8 * block : 8 * block + rows]
+        return tuple(carry)
+
+    for i in range(pieces):
+        crm_loads[i].wait()
+        sums = lax.fori_loop(i * CX // pieces, (i + 1) * CX // pieces, relayout, sums)
+    for half in range(2):
+        levels = slice(half * ZROWS, half * ZROWS + CZ)
+        average = sums[half] * (1.0 / CX)
+        mean[levels, :] = average
+        spread[levels, :] = sums[2 + half] * (1.0 / CX) - average * average
+
+    settle(1)
     new[0, :, 2 * L :] = step(slice(2 * L, FL))
 
     count = active[...]
@@ -213,30 +259,6 @@
     weights[L : L + CZ, L : 2 * L] = vmap[...]
     delta[...] = jnp.zeros((CPD, SLOTS), jnp.float32)
 
-    sums = tuple(jnp.zeros((CZ, HALF), jnp.float32) for _ in range(4))
-
-    def relayout(column, carry):
-        carry = list(carry)
-        spot = lax.rem(column, 8) * 8 + column // 8
-        for half in range(2):
-            start = pl.multiple_of(column * SLOTS + half * HALF, HALF)
-            values = crm[:, pl.ds(start, HALF)].astype(jnp.float32)
-            carry[half] = carry[half] + values
-            carry[2 + half] = carry[2 + half] + values * values
-            for block in range(ZROWS // 8):
-                rows = min(8, CZ - 8 * block)
-                field[pl.ds(half * HROWS + block * 8 * CX + spot, rows, stride=CX), :] = values[8 * block : 8 * block + rows]
-        return tuple(carry)
-
-    for i in range(pieces):
-        crm_loads[i].wait()
-        sums = lax.fori_loop(i * CX // pieces, (i + 1) * CX // pieces, relayout, sums)
-    for half in range(2):
-        levels = slice(half * ZROWS, half * ZROWS + CZ)
-        average = sums[half] * (1.0 / CX)
-        mean[levels, :] = average
-        spread[levels, :] = sums[2 + half] * (1.0 / CX) - average * average
-
     for half in range(2):
         lanes = slice(half * HALF, (half + 1) * HALF)
         base = half * HROWS
@@ -244,9 +266,7 @@
         arrived = recv.at[pl.ds(half * N // 2, N // 2)]
         pltpu.make_async_copy(arrived, arrived, fwd_recv.at[half]).wait()
         columns = recv[half * N // 2 : (half + 1) * N // 2].reshape(HALF, 2 * L)
-        both = lax.dot_general(
-            weights[...], columns, (((1,), (1,)), ((), ())), precision=HIGHEST, preferred_element_type=jnp.float32
-        )
+        both = product(weights[...], columns, 1, 1)
         forcing = both[0:CZ]
         courant = max_courant * jax.nn.sigmoid(both[L : L + CZ])
         keep = 1.0 - courant
@@ -295,9 +315,9 @@
             return carry
 
         none = jnp.zeros((CX, HALF), jnp.float32)
-        lax.fori_loop(0, CZ, up_sweep, none)
-        lax.fori_loop(0, CZ, down_sweep, (none, none))
-        lax.fori_loop(0, CZ, last_sweep, none)
+        lax.fori_loop(0, CZ, up_sweep, none, unroll=UNROLL)
+        lax.fori_loop(0, CZ, down_sweep, (none, none), unroll=UNROLL)
+        lax.fori_loop(0, CZ, last_sweep, none, unroll=UNROLL)
 
         def level_sums(ref):
             blocks = []
@@ -313,9 +333,7 @@
         spread_after = level_sums(partsq) - mean_after * mean_after
         delta[0:CZ, lanes] = mean_after - mean[levels, :]
         delta[L : L + CZ, lanes] = spread_after - spread[levels, :]
-        tend = lax.dot_general(
-            delta[:, lanes], weights[...], (((0,), (0,)), ((), ())), precision=HIGHEST, preferred_element_type=jnp.float32
-        )
+        tend = product(delta[:, lanes], weights[...], 0, 0)
         reply[half * N // 2 : (half + 1) * N // 2] = tend.reshape(N // 2, 2, 2 * L)
 
         targets = [xt * (NZ * NC) + ct for xt in (2 * half, 2 * half + 1) for ct in range(NC)]
@@ -412,8 +430,8 @@
             pltpu.SemaphoreType.REGULAR,
             dma((6,)),
             dma((4,)),
-            dma((2,)),
-            dma((2,)),
+            dma((4,)),
+            dma((4,)),
             dma,
             dma((2,)),
             dma,

time: 45.6 us -> 42.5 us (0.932)
  Pallas kernels: 44.7 us -> 41.8 us
    pallas_call x1, Pallas kernels: 43.2 us -> 40.3 us  [shards(): pl.pallas_call(kernel, out_shape=(pltpu.VMEM(state.shape, f32), pltpu.VME...]
where the time goes in v3:
time: 42.5 us; the launch traced here: 42.4 us
  Pallas kernels  41.8 us (98%)
  between operations  0.64 us (2%)
    pallas_call x1, Pallas kernels, shards(): pl.pallas_call(kernel, out_shape=(pltpu.VMEM(state.shape, f32), pltpu.VME...  40.3 us
    pallas_call x1, Pallas kernels, shards(): pl.pallas_call(ship, out_shape=(pltpu.HBM(state.shape, f32), pltpu.HBM(cr...  1.47 us

profile of v3, /device:TPU:7, one launch (start us, length us, event | category | flops | bytes accessed | tf_op | source)
XLA Modules:
  0.0 42.4 jit_solution(14384581305106469978)
XLA Ops:
  0.6 40.3 %shard_map.86 = (f32[1,128,512]{2,1,0:T(8,128)S(1)}, bf16[1,1,58,16384]{3,2,1,0:T(8,128)(2,1)S(1)}) custom-call(f32[1,128,512]{2,1,0:T(8,128)} %state_hbm.1, s32[1,128]{1,0:T(1,128)} %bitcast.5, s32[1,2]{1,0:T(1,128)} %bitcast.6, bf16[1,1,58,16384]{3,2,1,0:T(8,128)(2,1)} %crm_hbm.1, s32[1,256]{1,0:T(1,128)} %bitcast.4, f32[58,64]{1,0:T(8,128)} %vmap_hbm.1, ...), custom_call_target="tpu_custom_call" | custom-call | tf_op jit(solution)/shard_map/pallas_call | solution.py:401
  40.9 1.5 %shard_map.87 = (f32[1,128,512]{2,1,0:T(8,128)}, bf16[1,1,58,16384]{3,2,1,0:T(8,128)(2,1)}) custom-call(f32[1,128,512]{2,1,0:T(8,128)S(1)} %get-tuple-element.4.new, bf16[1,1,58,16384]{3,2,1,0:T(8,128)(2,1)S(1)} %get-tuple-element.5.out), custom_call_target="tpu_custom_call" | custom-call | tf_op jit(solution)/shard_map/pallas_call | solution.py:450
